TPU v7x, 512 devices: a whole 4x4x16 slice. The times are simulated.
512 devices in a mesh: tok: 16 (over y, x), hid: 32 (over z, core).
Axes of the slice: x: 4, y: 4, z: 16, core: 2. Of those that a mesh axis runs over, the one named last changes fastest.
Arguments:
- tokens: bfloat16 [2048, 8192], P('tok', 'hid'), may hold values from -6 to 6
- gate_weight: bfloat16 [8192, 16384], P('tok', 'hid'), may hold values from -0.09375 to 0.09375
- up_weight: bfloat16 [8192, 16384], P('tok', 'hid'), may hold values from -0.09375 to 0.09375
- down_weight: bfloat16 [16384, 8192], P('hid', 'tok'), may hold values from -0.0625 to 0.0625
- gate_keep: int32 [64, 128], P('tok', 'hid'), may hold values from 0 to 1, as said below
- up_keep: int32 [64, 128], P('tok', 'hid'), may hold values from 0 to 1, as said below
- down_keep: int32 [128, 64], P('hid', 'tok'), may hold values from 0 to 1, as said below
Outputs:
- mixed: bfloat16 [2048, 8192], P('hid', 'tok')
Inputs may be any that keep to these rules, and one draw needn't show every extreme that they name: `gate_keep`: in every device's shard of 4 x 4 blocks of a mask, between 4 and 8 blocks are kept; in every mask some shard keeps exactly 8. Shards of down_keep are 4 x 4. `up_keep`: as for gate_keep, drawn independently. `down_keep`: as for gate_keep, drawn independently.
All inputs are finite; a program needn't handle non-finite values.
Results may differ from a plain program's by a relative error of at most 0.0049.
Values may be sent and summed in bfloat16 or wider, within the bound.
A program may use at most 64 MiB of HBM per device.

v0:
```python
import jax
import jax.numpy as jnp
from jax import lax
from jax.sharding import PartitionSpec as P


def pack_blocks(weight, keep_mask):
    block_rows, block_cols = keep_mask.shape
    side = weight.shape[0] // block_rows
    capacity = block_rows * block_cols // 2
    flat_keep = keep_mask.reshape(-1)
    block_rank = jnp.cumsum(flat_keep) - 1
    slot_ids = jnp.arange(capacity, dtype=jnp.int32)
    select = ((block_rank[None, :] == slot_ids[:, None]) & (flat_keep[None, :] == 1)).astype(
        weight.dtype
    )
    blocks = weight.reshape(block_rows, side, block_cols, side).transpose(0, 2, 1, 3)
    blocks = blocks.reshape(block_rows * block_cols, side, side)
    packed = jnp.einsum("sb,bij->sij", select, blocks, preferred_element_type=jnp.float32)
    return (packed.astype(weight.dtype)[None], flat_keep[None])


def unpack_blocks(packed, flags, block_rows, block_cols):
    shards, capacity, side, _ = packed.shape
    block_rank = jnp.cumsum(flags, axis=1) - 1
    slot_ids = jnp.arange(capacity, dtype=jnp.int32)
    select = (
        (block_rank[:, :, None] == slot_ids[None, None, :]) & (flags[:, :, None] == 1)
    ).astype(packed.dtype)
    dense_tiles = jnp.einsum(
        "kbs,ksij->kbij", select, packed, preferred_element_type=jnp.float32
    ).astype(packed.dtype)
    dense_tiles = dense_tiles.reshape(shards, block_rows, block_cols, side, side).transpose(
        0, 1, 3, 2, 4
    )
    return dense_tiles.reshape(shards * block_rows * side, block_cols * side)


def prune_local(weight, keep_mask):
    block_rows, block_cols = keep_mask.shape
    row_count, col_count = weight.shape
    tiles = weight.reshape(block_rows, row_count // block_rows, block_cols, col_count // block_cols)
    kept = tiles * keep_mask[:, None, :, None].astype(weight.dtype)
    return kept.reshape(row_count, col_count)


def local(tokens, gate_weight, up_weight, down_weight, gate_keep, up_keep, down_keep):
    features_all = lax.all_gather(tokens, "hid", axis=1, tiled=True)
    block_rows, block_cols = gate_keep.shape
    gate_packed, gate_flags = pack_blocks(gate_weight, gate_keep)
    up_packed, up_flags = pack_blocks(up_weight, up_keep)

    def add_product(packed, flags):
        dense_strip = unpack_blocks(packed, flags, block_rows, block_cols)
        return jnp.dot(features_all, dense_strip, preferred_element_type=jnp.float32)

    def add_single(arrived):
        return add_product(arrived[0], arrived[1])

    gate_out = add_single(
        (
            lax.all_gather(gate_packed, "tok", axis=0, tiled=True),
            lax.all_gather(gate_flags, "tok", axis=0, tiled=True),
        )
    )
    up_out = add_single(
        (
            lax.all_gather(up_packed, "tok", axis=0, tiled=True),
            lax.all_gather(up_flags, "tok", axis=0, tiled=True),
        )
    )
    hidden = (jax.nn.silu(gate_out) * up_out).astype(jnp.bfloat16)
    down_dense = prune_local(down_weight, down_keep)
    partial_sums = jnp.dot(
        lax.all_gather(hidden, "tok", axis=0, tiled=True),
        down_dense,
        preferred_element_type=jnp.float32,
    )
    mixed = lax.psum_scatter(partial_sums, "hid", scatter_dimension=0, tiled=True)
    return mixed.astype(jnp.bfloat16)


def solution(mesh):
    return jax.shard_map(
        local,
        mesh=mesh,
        in_specs=(
            P("tok", "hid"),
            P("tok", "hid"),
            P("tok", "hid"),
            P("hid", "tok"),
            P("tok", "hid"),
            P("tok", "hid"),
            P("hid", "tok"),
        ),
        out_specs=P("hid", "tok"),
        check_vma=False,
    )
```

profile of v0, /device:TPU:2, one launch (start us, length us, event | category | flops | bytes accessed | tf_op | source)
XLA Modules:
  0.0 433.2 jit_solution(12943204567747657550)
XLA Ops:
  6.5 0.8 reshape.145
  7.4 0.7 broadcast_compare_fusion.3
  8.1 1.2 reshape.124
  9.2 0.2 copy.25
  9.4 0.1 add_reduce_fusion.1
  9.6 0.1 eq.90
  9.7 0.9 convolution_convert_fusion.3
  10.7 1.2 reshape.129
  11.8 0.2 copy.29
  12.2 0.1 eq.99
  12.3 0.1 add_reduce_fusion
  12.4 0.9 convolution_convert_fusion.2
  13.4 0.7 all-gather.9.cloned.1.call-update
  14.3 23.2 %all-gather.2 = s32[16,1,16]{2,1,0:T(1,128)S(1)} all-gather(s32[1,1,16]{2,1,0:T(1,128)S(1)} %reshape.135), channel_id=1, replica_groups=mesh['tok'=16,'hid'=32] {'tok'}, dimensions={0}, use_global_device_ids=true | all-gather | bytes 1088 | tf_op jit(solution)/shard_map/all_gather | solution.py:63
  37.4 0.2 reduce_window_sum.26
  37.6 18.3 %all-gather.3 = s32[16,1,16]{2,1,0:T(1,128)S(1)} all-gather(s32[1,1,16]{2,1,0:T(1,128)S(1)} %reshape.137), channel_id=1, replica_groups=mesh['tok'=16,'hid'=32] {'tok'}, dimensions={0}, use_global_device_ids=true | all-gather | bytes 1088 | tf_op jit(solution)/shard_map/all_gather | solution.py:69
  55.9 0.2 reduce_window_sum.27
  56.1 31.0 %all-gather.13.cloned.1.call-done = bf16[128,128,128]{2,0,1:T(8,128)(2,1)} async-done(((bf16[8,128,128]{2,0,1:T(8,128)(2,1)}), bf16[128,128,128]{2,0,1:T(8,128)(2,1)}) %all-gather.13.cloned.1.call-update) | async-done | bytes 4194320 | tf_op jit(solution)/shard_map/all_gather | solution.py:62
  87.1 4.2 convolution_convert_fusion.1
  91.3 5.9 %copy.27 = bf16[16,4,4,128,128]{4,2,3,1,0:T(4,128)(2,1)} copy(bf16[16,4,4,128,128]{4,2,1,3,0:T(4,128)(2,1)S(1)} %bitcast.70) | data formatting | bytes 16777216 | tf_op jit(solution)/shard_map/reshape | solution.py:33
  97.2 64.5 %all-gather.15.cloned.1.call-done = bf16[128,128,128]{2,0,1:T(8,128)(2,1)} async-done(((bf16[8,128,128]{2,0,1:T(8,128)(2,1)}), bf16[128,128,128]{2,0,1:T(8,128)(2,1)}) %all-gather.15.cloned.1.call-update) | async-done | bytes 4194320 | tf_op jit(solution)/shard_map/all_gather | solution.py:68
  161.7 4.2 convolution_convert_fusion
  165.9 5.9 %copy.31 = bf16[16,4,4,128,128]{4,2,3,1,0:T(4,128)(2,1)} copy(bf16[16,4,4,128,128]{4,2,1,3,0:T(4,128)(2,1)S(1)} %bitcast.71) | data formatting | bytes 16777216 | tf_op jit(solution)/shard_map/reshape | solution.py:33
  171.8 64.5 %all-gather.9.cloned.1.call-done = bf16[128,8192]{1,0:T(8,128)(2,1)} async-done(((bf16[128,256]{1,0:T(8,128)(2,1)}), bf16[128,8192]{1,0:T(8,128)(2,1)}) %all-gather.9.cloned.1.call-update) | async-done | bytes 2097168 | tf_op jit(solution)/shard_map/all_gather | solution.py:48
  236.4 6.5 %fusion.8 = f32[128,512]{0,1:T(8,128)S(1)} fusion(bf16[128,8192]{1,0:T(8,128)(2,1)} %all-gather.9.cloned.1.call-done, bf16[1024,8,4,128]{3,2,1,0:T(4,128)(2,1)} %bitcast.72), kind=kOutput, calls=%fused_computation.12 | convolution fusion | flops 1073741824 | bytes 10747904 | tf_op jit(solution)/shard_map/dot_general | solution.py:55
  242.8 0.5 copy-done.5
  243.3 3.3 fusion.17
  246.7 58.0 %all-gather.11.cloned.1.call-done = bf16[2048,512]{0,1:T(8,128)(2,1)} async-done(((bf16[128,512]{0,1:T(8,128)(2,1)}), bf16[2048,512]{0,1:T(8,128)(2,1)}) %all-gather.11.cloned.1.call-update) | async-done | bytes 2097168 | tf_op jit(solution)/shard_map/all_gather | solution.py:75
  304.6 0.2 mul.20
  304.8 4.8 %fusion.20 = f32[2048,512]{1,0:T(8,128)} fusion(bf16[2048,512]{0,1:T(8,128)(2,1)} %all-gather.11.cloned.1.call-done, bf16[512,512]{1,0:T(8,128)(2,1)S(1)} %copy-done.1, bf16[64,8,4,128]{3,2,1,0:T(4,128)(2,1)S(1)} %bitcast.74), kind=kOutput, calls=%fused_computation.17 | convolution fusion | flops 1074003968 | bytes 7340032 | tf_op jit(solution)/shard_map/dot_general | solution.py:74
  309.7 115.4 %reduce-scatter.2.cloned.1.call-done = f32[64,512]{1,0:T(8,128)} async-done(((f32[2048,512]{1,0:T(8,128)}), f32[64,512]{1,0:T(8,128)}) %reduce-scatter.2.cloned.1.call-update) | async-done | bytes 131088 | tf_op jit(solution)/shard_map/reduce_scatter | solution.py:79
  425.1 1.5 convert_element_type.32
  (31 shorter events, 0.6 us)
Async XLA Ops:
  6.5 7.6 %copy-start.2 = (s32[4,4]{1,0:T(4,128)S(1)}, s32[4,4]{1,0:T(4,128)}, u32[]{:S(2)}) copy-start(s32[4,4]{1,0:T(4,128)} %param.11) | copy-start | bytes 196
  6.5 5.5 %copy-start.3 = (s32[4,4]{1,0:T(4,128)S(1)}, s32[4,4]{1,0:T(4,128)}, u32[]{:S(2)}) copy-start(s32[4,4]{1,0:T(4,128)} %param.12) | copy-start | bytes 196
  6.5 80.5 %all-gather.13.cloned.1.call-start = ((), (), s32[]{:S(2)}) async-start(), calls=%async_computation.4 | async-start | bytes 4456448 | tf_op jit(solution)/shard_map/all_gather | solution.py:62
  10.6 151.0 %all-gather.15.cloned.1.call-start = ((), (), s32[]{:S(2)}) async-start(), calls=%async_computation.5 | async-start | bytes 4456448 | tf_op jit(solution)/shard_map/all_gather | solution.py:68
  13.3 223.0 %all-gather.9.cloned.1.call-start = ((), (), s32[]{:S(2)}) async-start(), calls=%async_computation.1 | async-start | bytes 2162688 | tf_op jit(solution)/shard_map/all_gather | solution.py:48
  14.1 290.6 %all-gather.11.cloned.1.call-start = ((), (), s32[]{:S(2)}) async-start(), calls=%async_computation.2 | async-start | bytes 2228224 | tf_op jit(solution)/shard_map/all_gather | solution.py:75
  236.4 6.5 %copy-start = (bf16[16,4,4,128,128]{4,2,3,1,0:T(4,128)(2,1)S(1)}, bf16[16,4,4,128,128]{4,2,3,1,0:T(4,128)(2,1)}, u32[]{:S(2)}) copy-start(bf16[16,4,4,128,128]{4,2,3,1,0:T(4,128)(2,1)} %copy.31) | copy-start | bytes 25165828
  236.4 7.0 %copy-start.5 = (bf16[128,8192]{1,0:T(8,128)(2,1)S(1)}, bf16[128,8192]{1,0:T(8,128)(2,1)}, u32[]{:S(2)}) copy-start(bf16[128,8192]{1,0:T(8,128)(2,1)} %all-gather.9.cloned.1.call-done) | copy-start | bytes 6291460
  243.3 3.3 copy-start.4
  243.3 61.5 %copy-start.1 = (bf16[512,512]{1,0:T(8,128)(2,1)S(1)}, bf16[512,512]{1,0:T(8,128)(2,1)}, u32[]{:S(2)}) copy-start(bf16[512,512]{1,0:T(8,128)(2,1)} %param.10) | copy-start | bytes 1572868
  246.6 178.5 %reduce-scatter.2.cloned.1.call-start = ((), (), s32[]{:S(2)}) async-start(), calls=%async_computation.3 | async-start | bytes 4325376 | tf_op jit(solution)/shard_map/reduce_scatter | solution.py:79
Sparse Core Ops, SparseCore 0:
  10.7 76.2 all-gather.12
  90.0 71.5 all-gather.14
  163.7 72.5 all-gather.8
  246.7 57.8 all-gather.10
  309.8 115.2 reduce-scatter.1
where the time goes:
time: 434 us; the launch traced here: 433 us
  waiting for transfers between devices  334 us (77%)
  blocking collectives  41.4 us (10%)
  matrix products  24.9 us (6%)
  local copies, waits for them, and re-layouts  16.4 us (4%)
  between operations  13.3 us (3%)
    reduce_scatter x1, waiting for transfers between devices, local(): lax.psum_scatter(partial_sums, 'hid', scatter_dimension=0, tiled=True)  115 us
    all_gather x1, waiting for transfers between devices, local(): features_all = lax.all_gather(tokens, 'hid', axis=1, tiled=True)  64.5 us
    all_gather x1, waiting for transfers between devices, local(): lax.all_gather(up_packed, 'tok', axis=0, tiled=True)  64.5 us
    all_gather x1, waiting for transfers between devices, local(): lax.all_gather(hidden, 'tok', axis=0, tiled=True)  58 us
    all_gather x1, waiting for transfers between devices, local(): lax.all_gather(gate_packed, 'tok', axis=0, tiled=True)  31 us
    all_gather x1, blocking collectives, local(): lax.all_gather(gate_flags, 'tok', axis=0, tiled=True)  23.2 us
    all_gather x1, blocking collectives, local(): lax.all_gather(up_flags, 'tok', axis=0, tiled=True)  18.3 us
    reshape x2, local copies, waits for them, and re-layouts, unpack_blocks(): dense_tiles.reshape(shards, block_rows, block_cols, side, side)  11.8 us
  transfers between devices with their start and end apart: 5, of which 5 were waited for; matrix products, arithmetic and copies ran while one was open for 5% of the time, Pallas kernels for 0%

commit v1 on v0

--- a/solution.py
+++ b/solution.py
@@ -65,7 +65,9 @@
     )
     up_out = add_single(
         (
-            lax.all_gather(up_packed, "tok", axis=0, tiled=True),
+            jnp.concatenate(
+                lax.all_to_all(jnp.stack([up_packed] * lax.axis_size("tok")), "tok", 0, 0), axis=0
+            ),
             lax.all_gather(up_flags, "tok", axis=0, tiled=True),
         )
     )

time: 434 us -> 397 us (0.915)
  the two profiles are of different devices: /device:TPU:2 before, /device:TPU:14 now
where the time goes in v1:
time: 397 us; the launch traced here: 396 us
  waiting for transfers between devices  242 us (61%)
  blocking collectives  84.9 us (21%)
  matrix products  24.1 us (6%)
  local copies, waits for them, and re-layouts  19.1 us (5%)
  between operations  13.3 us (3%)
  starting transfers between devices  10.3 us (3%)
    reduce_scatter x1, waiting for transfers between devices, local(): lax.psum_scatter(partial_sums, 'hid', scatter_dimension=0, tiled=True)  117 us
    all_gather x1, waiting for transfers between devices, local(): features_all = lax.all_gather(tokens, 'hid', axis=1, tiled=True)  65.8 us
    all_gather x1, blocking collectives, local(): lax.all_gather(gate_flags, 'tok', axis=0, tiled=True)  65.5 us
    all_gather x1, waiting for transfers between devices, local(): lax.all_gather(hidden, 'tok', axis=0, tiled=True)  56.7 us
    all_gather x1, blocking collectives, local(): lax.all_gather(up_flags, 'tok', axis=0, tiled=True)  19.4 us
    reshape x2, local copies, waits for them, and re-layouts, unpack_blocks(): dense_tiles.reshape(shards, block_rows, block_cols, side, side)  11.8 us
    all_to_all x1, starting transfers between devices, local(): lax.all_to_all(jnp.stack([up_packed] * lax.axis_size('tok')), 'tok', 0, 0)  10.1 us
    dot_general x2, matrix products, add_product(): jnp.dot(features_all, dense_strip, preferred_element_type=jnp.float32)  9.72 us
  transfers between devices with their start and end apart: 5, of which 4 were waited for; matrix products, arithmetic and copies ran while one was open for 6% of the time, Pallas kernels for 0%

profile of v1, /device:TPU:14, one launch (start us, length us, event | category | flops | bytes accessed | tf_op | source)
XLA Modules:
  0.0 396.5 jit_solution(8444089440708936000)
XLA Ops:
  6.5 0.8 reshape.150
  7.3 0.7 broadcast_compare_fusion.3
  8.0 1.2 reshape.129
  9.2 0.2 copy.23
  9.4 0.1 add_reduce_fusion.1
  9.6 0.9 convolution_convert_fusion.3
  10.5 1.2 reshape.134
  11.7 0.2 copy.27
  12.0 0.1 eq.99
  12.1 0.1 add_reduce_fusion
  12.2 0.2 convolution_convert_fusion.2
  12.5 2.8 stack.3
  15.2 10.1 %all-to-all-start = ((bf16[16,1,8,128,128]{4,2,3,1,0:T(8,128)(2,1)}), bf16[16,1,8,128,128]{4,2,3,1,0:T(8,128)(2,1)}, u32[]{:S(2)}, u32[]{:S(2)}) async-start(bf16[16,1,8,128,128]{4,2,3,1,0:T(8,128)(2,1)} %stack.3), calls=%async_computation | async-start | bytes 8388608 | tf_op jit(solution)/shard_map/all_to_all | solution.py:69
  25.4 0.7 all-gather.7.cloned.1.call-update
  26.4 65.5 %all-gather.1 = s32[16,1,16]{2,1,0:T(1,128)S(1)} all-gather(s32[1,1,16]{2,1,0:T(1,128)S(1)} %reshape.140), channel_id=1, replica_groups=mesh['tok'=16,'hid'=32] {'tok'}, dimensions={0}, use_global_device_ids=true | all-gather | bytes 1088 | tf_op jit(solution)/shard_map/all_gather | solution.py:63
  91.9 0.2 reduce_window_sum.26
  92.1 19.4 %all-gather.2 = s32[16,1,16]{2,1,0:T(1,128)S(1)} all-gather(s32[1,1,16]{2,1,0:T(1,128)S(1)} %reshape.142), channel_id=1, replica_groups=mesh['tok'=16,'hid'=32] {'tok'}, dimensions={0}, use_global_device_ids=true | all-gather | bytes 1088 | tf_op jit(solution)/shard_map/all_gather | solution.py:71
  111.5 0.2 reduce_window_sum.27
  111.7 4.2 %convolution_convert_fusion = bf16[16,16,128,128]{3,1,2,0:T(8,128)(2,1)S(1)} fusion(bf16[16,1,8,128,128]{4,2,3,1,0:T(8,128)(2,1)} %all-to-all-done, s32[16,16]{1,0:T(8,128)S(1)} %broadcast_add_fusion, pred[16,16]{1,0:T(8,128)(4,1)S(1)} %broadcast_compare_fusion), kind=kOutput, calls=%fused_computation.6 | convolution fusion | flops 71307264 | bytes 12584192 | tf_op jit(solution)/shard_map/kbs,ksij->kbij/dot_general | solution.py:30
  115.9 5.8 %copy.28 = bf16[16,4,4,128,128]{4,2,3,1,0:T(4,128)(2,1)} copy(bf16[16,4,4,128,128]{4,2,1,3,0:T(4,128)(2,1)S(1)} %bitcast.69) | data formatting | bytes 16777216 | tf_op jit(solution)/shard_map/reshape | solution.py:33
  121.7 2.0 all-gather.11.cloned.1.call-done
  123.7 4.2 %convolution_convert_fusion.1 = bf16[16,16,128,128]{3,1,2,0:T(8,128)(2,1)S(1)} fusion(s32[16,16]{1,0:T(8,128)S(1)} %broadcast_add_fusion.1, pred[16,16]{1,0:T(8,128)(4,1)S(1)} %broadcast_compare_fusion.1, bf16[128,128,128]{2,0,1:T(8,128)(2,1)} %all-gather.11.cloned.1.call-done), kind=kOutput, calls=%fused_computation.7 | convolution fusion | flops 71307264 | bytes 12584192 | tf_op jit(solution)/shard_map/kbs,ksij->kbij/dot_general | solution.py:30
  128.0 5.9 %copy.25 = bf16[16,4,4,128,128]{4,2,3,1,0:T(4,128)(2,1)} copy(bf16[16,4,4,128,128]{4,2,1,3,0:T(4,128)(2,1)S(1)} %bitcast.70) | data formatting | bytes 16777216 | tf_op jit(solution)/shard_map/reshape | solution.py:33
  133.9 65.8 %all-gather.7.cloned.1.call-done = bf16[128,8192]{1,0:T(8,128)(2,1)} async-done(((bf16[128,256]{1,0:T(8,128)(2,1)}), bf16[128,8192]{1,0:T(8,128)(2,1)}) %all-gather.7.cloned.1.call-update) | async-done | bytes 2097168 | tf_op jit(solution)/shard_map/all_gather | solution.py:48
  199.7 6.5 %fusion.8 = f32[128,512]{0,1:T(8,128)S(1)} fusion(bf16[128,8192]{1,0:T(8,128)(2,1)} %all-gather.7.cloned.1.call-done, bf16[1024,8,4,128]{3,2,1,0:T(4,128)(2,1)} %bitcast.72), kind=kOutput, calls=%fused_computation.12 | convolution fusion | flops 1073741824 | bytes 10747904 | tf_op jit(solution)/shard_map/dot_general | solution.py:55
  206.2 0.5 copy-done.5
  206.6 3.2 fusion.17
  210.0 56.7 %all-gather.9.cloned.1.call-done = bf16[2048,512]{0,1:T(8,128)(2,1)} async-done(((bf16[128,512]{0,1:T(8,128)(2,1)}), bf16[2048,512]{0,1:T(8,128)(2,1)}) %all-gather.9.cloned.1.call-update) | async-done | bytes 2097168 | tf_op jit(solution)/shard_map/all_gather | solution.py:77
  266.7 0.2 mul.20
  266.9 4.8 %fusion.20 = f32[2048,512]{1,0:T(8,128)} fusion(bf16[2048,512]{0,1:T(8,128)(2,1)} %all-gather.9.cloned.1.call-done, bf16[512,512]{1,0:T(8,128)(2,1)S(1)} %copy-done.1, bf16[64,8,4,128]{3,2,1,0:T(4,128)(2,1)S(1)} %bitcast.73), kind=kOutput, calls=%fused_computation.17 | convolution fusion | flops 1074003968 | bytes 7340032 | tf_op jit(solution)/shard_map/dot_general | solution.py:76
  271.7 116.7 %reduce-scatter.2.cloned.1.call-done = f32[64,512]{1,0:T(8,128)} async-done(((f32[2048,512]{1,0:T(8,128)}), f32[64,512]{1,0:T(8,128)}) %reduce-scatter.2.cloned.1.call-update) | async-done | bytes 131088 | tf_op jit(solution)/shard_map/reduce_scatter | solution.py:81
  388.4 1.5 convert_element_type.32
  (31 shorter events, 0.6 us)
Async XLA Ops:
  6.5 5.4 %copy-start.3 = (s32[4,4]{1,0:T(4,128)S(1)}, s32[4,4]{1,0:T(4,128)}, u32[]{:S(2)}) copy-start(s32[4,4]{1,0:T(4,128)} %param.12) | copy-start | bytes 196
  6.5 117.2 %all-gather.11.cloned.1.call-start = ((), (), s32[]{:S(2)}) async-start(), calls=%async_computation.5 | async-start | bytes 4456448 | tf_op jit(solution)/shard_map/all_gather | solution.py:62
  15.2 10.9 %copy-start.2 = (s32[4,4]{1,0:T(4,128)S(1)}, s32[4,4]{1,0:T(4,128)}, u32[]{:S(2)}) copy-start(s32[4,4]{1,0:T(4,128)} %param.11) | copy-start | bytes 196
  15.2 96.4 %all-to-all-start = ((bf16[16,1,8,128,128]{4,2,3,1,0:T(8,128)(2,1)}), bf16[16,1,8,128,128]{4,2,3,1,0:T(8,128)(2,1)}, u32[]{:S(2)}, u32[]{:S(2)}) async-start(bf16[16,1,8,128,128]{4,2,3,1,0:T(8,128)(2,1)} %stack.3), calls=%async_computation | async-start | bytes 8388608 | tf_op jit(solution)/shard_map/all_to_all | solution.py:69
  25.4 174.3 %all-gather.7.cloned.1.call-start = ((), (), s32[]{:S(2)}) async-start(), calls=%async_computation.2 | async-start | bytes 2162688 | tf_op jit(solution)/shard_map/all_gather | solution.py:48
  26.1 240.5 %all-gather.9.cloned.1.call-start = ((), (), s32[]{:S(2)}) async-start(), calls=%async_computation.3 | async-start | bytes 2228224 | tf_op jit(solution)/shard_map/all_gather | solution.py:77
  199.7 6.5 %copy-start = (bf16[16,4,4,128,128]{4,2,3,1,0:T(4,128)(2,1)S(1)}, bf16[16,4,4,128,128]{4,2,3,1,0:T(4,128)(2,1)}, u32[]{:S(2)}) copy-start(bf16[16,4,4,128,128]{4,2,3,1,0:T(4,128)(2,1)} %copy.28) | copy-start | bytes 25165828
  199.7 7.0 %copy-start.5 = (bf16[128,8192]{1,0:T(8,128)(2,1)S(1)}, bf16[128,8192]{1,0:T(8,128)(2,1)}, u32[]{:S(2)}) copy-start(bf16[128,8192]{1,0:T(8,128)(2,1)} %all-gather.7.cloned.1.call-done) | copy-start | bytes 6291460
  206.6 3.3 copy-start.4
  206.6 60.2 %copy-start.1 = (bf16[512,512]{1,0:T(8,128)(2,1)S(1)}, bf16[512,512]{1,0:T(8,128)(2,1)}, u32[]{:S(2)}) copy-start(bf16[512,512]{1,0:T(8,128)(2,1)} %param.10) | copy-start | bytes 1572868
  209.9 178.5 %reduce-scatter.2.cloned.1.call-start = ((), (), s32[]{:S(2)}) async-start(), calls=%async_computation.4 | async-start | bytes 4325376 | tf_op jit(solution)/shard_map/reduce_scatter | solution.py:81
Sparse Core Ops, SparseCore 0:
  10.7 113.0 all-gather.10
  125.8 73.8 all-gather.6
  210.0 56.6 all-gather.8
  271.9 116.5 reduce-scatter.1
